TPU v7x, 32 devices: a whole 2x2x4 slice. The times are simulated.
32 devices in a mesh: dp: 16 (over z, y, x), tensor: 2 (over core).
Axes of the slice: x: 2, y: 2, z: 4, core: 2. Of those that a mesh axis runs over, the one named last changes fastest.
Arguments:
- tokens: bfloat16 [8192, 1024], P(('dp', 'tensor')), may hold values from -6 to 6
- teacher: bfloat16 [8192, 1024], P(('dp', 'tensor')), may hold values from -6 to 6
- lengths: int32 [16], P('dp'), may hold values from 128 to 512, as said below
- w_qkv: bfloat16 [1024, 3, 1024], P('dp', None, 'tensor'), may hold values from -0.1875 to 0.1875
- w_out: bfloat16 [1024, 1024], P('dp', 'tensor'), may hold values from -0.1875 to 0.1875
- w_up: bfloat16 [1024, 4096], P('dp', 'tensor'), may hold values from -0.1875 to 0.1875
- w_down: bfloat16 [1024, 4096], P('dp', 'tensor'), may hold values from -0.09375 to 0.09375
- norm_gain: float32 [4, 1024], replicated, may hold values from 0.5 to 1.5
- norm_bias: float32 [4, 1024], replicated, may hold values from -3 to 3
Outputs:
- loss: float32 [], replicated
- layer_output: bfloat16 [8192, 1024], P(('dp', 'tensor'))
- tokens_grad: float32 [8192, 1024], P(('dp', 'tensor'))
- w_qkv_grad: float32 [1024, 3, 1024], P('dp', None, 'tensor')
- w_out_grad: float32 [1024, 1024], P('dp', 'tensor')
- w_up_grad: float32 [1024, 4096], P('dp', 'tensor')
- w_down_grad: float32 [1024, 4096], P('dp', 'tensor')
- gain_grad: float32 [4, 1024], P(None, ('dp', 'tensor'))
- bias_grad: float32 [4, 1024], P(None, ('dp', 'tensor'))
Inputs may be any that keep to these rules, and one draw needn't show every extreme that they name: Each row's valid slots are its first lengths[r] slots.
All inputs are finite; a program needn't handle non-finite values.
Results may differ from a plain program's by a relative error of at most 0.015.
Values may be sent and summed in bfloat16 or wider, within the bound.
No kernel may reach another device: no remote copies, remote signals or barrier semaphores. Data moves between devices by JAX's collectives and lax.ppermute only.
A program may use at most 128 MiB of HBM per device.

v0:
```python
import jax
import jax.numpy as jnp
from jax import lax
from jax.sharding import PartitionSpec as P

HEAD_DIM = 64


norm_eps = 1e-05


def layer_norm(values, gain, shift):
    center = values - jnp.mean(values, axis=-1, keepdims=True)
    spread = jnp.mean(center * center, axis=-1, keepdims=True)
    return center * lax.rsqrt(spread + norm_eps) * gain + shift


def rotary_tables(slot_count, head_size):
    places = jnp.arange(slot_count).astype(jnp.float32)
    freqs = 10000.0 ** (-2.0 * jnp.arange(head_size // 2).astype(jnp.float32) / head_size)
    angles = places[:, None] * freqs[None, :]
    return (jnp.cos(angles)[:, None, :], jnp.sin(angles)[:, None, :])


def rotate_pairs(values, cosine, sine):
    half_size = values.shape[-1] // 2
    front = values[..., :half_size]
    back_half = values[..., half_size:]
    return jnp.concatenate(
        [front * cosine - back_half * sine, back_half * cosine + front * sine], axis=-1
    )


def allowed_pairs(begin, block, key_count, length):
    key_places = jnp.arange(key_count)
    query_places = begin + jnp.arange(block)
    return (key_places[None, :] <= query_places[:, None]) & (key_places[None, :] < length)


def attend_forward(packed):
    queries, key_rows, value_rows, length = packed
    slot_count = queries.shape[0]
    block = min(512, slot_count)
    scale = HEAD_DIM ** (-0.5)
    outputs = []
    totals = []
    for begin in range(0, slot_count, block):
        finish = begin + block
        scores = (
            jnp.einsum(
                "qhd,khd->hqk",
                queries[begin:finish],
                key_rows[:finish],
                preferred_element_type=jnp.float32,
            )
            * scale
        )
        allowed = allowed_pairs(begin, block, finish, length)
        scores = jnp.where(allowed[None], scores, -1000000000.0)
        top_score = jnp.max(scores, axis=-1, keepdims=True)
        weights = jnp.exp(scores - top_score)
        weight_sum = jnp.sum(weights, axis=-1, keepdims=True)
        probs = (weights / weight_sum).astype(jnp.bfloat16)
        outputs.append(
            jnp.einsum(
                "hqk,khd->qhd", probs, value_rows[:finish], preferred_element_type=jnp.float32
            )
        )
        totals.append((top_score + jnp.log(weight_sum))[:, :, 0])
    return (jnp.concatenate(outputs, axis=0), jnp.concatenate(totals, axis=1))


def attend_backward(packed):
    queries, key_rows, value_rows, outputs, out_grads, totals, length = packed
    slot_count = queries.shape[0]
    block = min(512, slot_count)
    scale = HEAD_DIM ** (-0.5)
    delta = jnp.sum(out_grads.astype(jnp.float32) * outputs, axis=-1).T
    key_grads = jnp.zeros(key_rows.shape, jnp.float32)
    value_grads = jnp.zeros(value_rows.shape, jnp.float32)
    query_grads = []
    for begin in range(0, slot_count, block):
        finish = begin + block
        query_block = queries[begin:finish]
        grad_block = out_grads[begin:finish]
        key_part = key_rows[:finish]
        value_part = value_rows[:finish]
        scores = (
            jnp.einsum("qhd,khd->hqk", query_block, key_part, preferred_element_type=jnp.float32)
            * scale
        )
        allowed = allowed_pairs(begin, block, finish, length)
        probs = jnp.where(allowed[None], jnp.exp(scores - totals[:, begin:finish, None]), 0.0)
        value_grads = value_grads.at[:finish].add(
            jnp.einsum(
                "hqk,qhd->khd",
                probs.astype(jnp.bfloat16),
                grad_block,
                preferred_element_type=jnp.float32,
            )
        )
        prob_grads = jnp.einsum(
            "qhd,khd->hqk", grad_block, value_part, preferred_element_type=jnp.float32
        )
        score_grads = (probs * (prob_grads - delta[:, begin:finish, None])).astype(jnp.bfloat16)
        query_grads.append(
            jnp.einsum("hqk,khd->qhd", score_grads, key_part, preferred_element_type=jnp.float32)
            * scale
        )
        key_grads = key_grads.at[:finish].add(
            jnp.einsum("hqk,qhd->khd", score_grads, query_block, preferred_element_type=jnp.float32)
            * scale
        )
    return (jnp.concatenate(query_grads, axis=0), key_grads, value_grads)


def collect_rows(values):
    return lax.all_gather(values, "tensor", axis=0, tiled=True)


def collect_grads(values):
    return lax.all_gather(values, "tensor", axis=0, tiled=True)


def branch_reduce(inputs, weight_t, form, own_rows):
    rows_in = lax.dynamic_slice_in_dim(inputs, jnp.int32(0), own_rows * lax.axis_size("tensor"), 0)
    return lax.psum_scatter(
        jnp.einsum(form, rows_in, weight_t, preferred_element_type=jnp.float32).astype(
            jnp.bfloat16
        ),
        "tensor",
        scatter_dimension=0,
        tiled=True,
    ).astype(jnp.float32)


def grad_reduce(inputs, weight_t, form, own_rows):
    rows_in = lax.dynamic_slice_in_dim(inputs, jnp.int32(0), own_rows * lax.axis_size("tensor"), 0)
    return lax.psum_scatter(
        jnp.einsum(form, rows_in, weight_t, preferred_element_type=jnp.float32).astype(
            jnp.bfloat16
        ),
        "tensor",
        scatter_dimension=0,
        tiled=True,
    ).astype(jnp.float32)


def on_device(tokens, teacher, lengths, w_qkv, w_out, w_up, w_down, norm_gain, norm_bias):
    tok_dev, width = tokens.shape
    groups = lax.axis_size("tensor")
    members = lax.axis_size("dp")
    row_count = lengths.shape[0]
    group_tokens = tok_dev * groups
    slot_count = group_tokens // row_count
    all_slots = group_tokens * members
    places = lax.axis_index("tensor") * tok_dev + jnp.arange(tok_dev)
    row_index = places // slot_count
    row_length = jnp.sum(
        jnp.where(row_index[:, None] == jnp.arange(row_count)[None, :], lengths[None, :], 0), axis=1
    )
    valid = (places % slot_count < row_length).astype(jnp.float32)[:, None]
    inputs = tokens.astype(jnp.float32)
    cosine, sine = rotary_tables(slot_count, HEAD_DIM)
    weight_qkv, weight_out, weight_up, weight_down = (
        lax.all_gather(w_qkv, "dp", axis=0, tiled=True),
        lax.all_gather(w_out, "dp", axis=0, tiled=True),
        lax.all_gather(w_up, "dp", axis=0, tiled=True),
        lax.all_gather(w_down, "dp", axis=0, tiled=True),
    )
    normed_one = layer_norm(inputs, norm_gain[0], norm_bias[0]).astype(jnp.bfloat16)
    rows_one = collect_rows(normed_one)
    mixed = jnp.einsum("td,dcf->tcf", rows_one, weight_qkv, preferred_element_type=jnp.float32)
    local_width = weight_qkv.shape[2]
    heads_here = local_width // HEAD_DIM
    mixed = mixed.reshape(row_count, slot_count, 3, heads_here, HEAD_DIM)
    queries = rotate_pairs(mixed[:, :, 0], cosine, sine).astype(jnp.bfloat16)
    key_rows = rotate_pairs(mixed[:, :, 1], cosine, sine).astype(jnp.bfloat16)
    value_rows = mixed[:, :, 2].astype(jnp.bfloat16)
    attended, totals = lax.map(attend_forward, (queries, key_rows, value_rows, lengths))
    attended_low = attended.reshape(group_tokens, local_width).astype(jnp.bfloat16)
    attn_sum = branch_reduce(attended_low, weight_out, "tk,dk->td", tok_dev)
    middle = inputs + layer_norm(attn_sum, norm_gain[1], norm_bias[1])
    normed_two = layer_norm(middle, norm_gain[2], norm_bias[2]).astype(jnp.bfloat16)
    rows_two = collect_rows(normed_two)
    hidden = jnp.dot(rows_two, weight_up, preferred_element_type=jnp.float32)
    active = jax.nn.gelu(hidden, approximate=False).astype(jnp.bfloat16)
    mlp_sum = branch_reduce(active, weight_down, "tk,dk->td", tok_dev)
    result = middle + layer_norm(mlp_sum, norm_gain[3], norm_bias[3])
    error = result - teacher.astype(jnp.float32)
    own_squared = jnp.sum(valid * error * error)
    squared, count = lax.psum((own_squared, jnp.sum(valid)), ("dp", "tensor"))
    loss = squared / (count * width)
    out_grad = valid * error * (all_slots / count)
    weight_qkv, weight_out, weight_up, weight_down = (
        lax.all_gather(w_qkv, "dp", axis=0, tiled=True),
        lax.all_gather(w_out, "dp", axis=0, tiled=True),
        lax.all_gather(w_up, "dp", axis=0, tiled=True),
        lax.all_gather(w_down, "dp", axis=0, tiled=True),
    )
    rows_one, rows_two = (
        lax.all_gather(normed_one, "tensor", axis=0, tiled=True),
        lax.all_gather(normed_two, "tensor", axis=0, tiled=True),
    )
    _, back_three = jax.vjp(layer_norm, mlp_sum, norm_gain[3], norm_bias[3])
    mlp_grad, gain_three, bias_three = back_three(out_grad)
    mlp_rows = collect_grads(mlp_grad.astype(jnp.bfloat16))
    active_grad = jnp.dot(mlp_rows, weight_down, preferred_element_type=jnp.float32)
    down_grad = jnp.einsum("td,tf->df", mlp_rows, active, preferred_element_type=jnp.float32)
    _, back_gelu = jax.vjp(lambda inner: jax.nn.gelu(inner, approximate=False), hidden)
    hidden_grad = back_gelu(active_grad)[0].astype(jnp.bfloat16)
    up_grad = jnp.einsum("td,tf->df", rows_two, hidden_grad, preferred_element_type=jnp.float32)
    normed_two_grad = grad_reduce(hidden_grad, weight_up, "tf,df->td", tok_dev)
    _, back_two = jax.vjp(layer_norm, middle, norm_gain[2], norm_bias[2])
    middle_extra, gain_two, bias_two = back_two(normed_two_grad)
    middle_grad = out_grad + middle_extra
    _, back_one = jax.vjp(layer_norm, attn_sum, norm_gain[1], norm_bias[1])
    attn_grad, gain_one, bias_one = back_one(middle_grad)
    attn_rows = collect_grads(attn_grad.astype(jnp.bfloat16))
    attended_grad = jnp.dot(attn_rows, weight_out, preferred_element_type=jnp.float32).astype(
        jnp.bfloat16
    )
    out_weight_grad = jnp.einsum(
        "td,tk->dk", attn_rows, attended_low, preferred_element_type=jnp.float32
    )
    attended_grad = attended_grad.reshape(row_count, slot_count, heads_here, HEAD_DIM)
    query_grads, key_grads, value_grads = lax.map(
        attend_backward, (queries, key_rows, value_rows, attended, attended_grad, totals, lengths)
    )
    mixed_grad = jnp.stack(
        [
            rotate_pairs(query_grads, cosine, -sine),
            rotate_pairs(key_grads, cosine, -sine),
            value_grads,
        ],
        axis=2,
    )
    mixed_grad = mixed_grad.reshape(group_tokens, 3, local_width).astype(jnp.bfloat16)
    qkv_grad = jnp.einsum("td,tcf->dcf", rows_one, mixed_grad, preferred_element_type=jnp.float32)
    normed_one_grad = grad_reduce(mixed_grad, weight_qkv, "tcf,dcf->td", tok_dev)
    _, back_zero = jax.vjp(layer_norm, inputs, norm_gain[0], norm_bias[0])
    input_extra, gain_zero, bias_zero = back_zero(normed_one_grad)
    tokens_grad = middle_grad + input_extra
    qkv_part, out_part, up_part, down_part = (
        lax.psum_scatter(
            qkv_grad.astype(jnp.bfloat16), "dp", scatter_dimension=0, tiled=True
        ).astype(jnp.float32),
        lax.psum_scatter(
            out_weight_grad.astype(jnp.bfloat16), "dp", scatter_dimension=0, tiled=True
        ).astype(jnp.float32),
        lax.psum_scatter(
            up_grad.astype(jnp.bfloat16), "dp", scatter_dimension=0, tiled=True
        ).astype(jnp.float32),
        lax.psum_scatter(
            down_grad.astype(jnp.bfloat16), "dp", scatter_dimension=0, tiled=True
        ).astype(jnp.float32),
    )
    gain_stack = jnp.stack([gain_zero, gain_one, gain_two, gain_three], axis=0)
    bias_stack = jnp.stack([bias_zero, bias_one, bias_two, bias_three], axis=0)
    gain_part, bias_part = (
        lax.psum_scatter(gain_stack, ("dp", "tensor"), scatter_dimension=1, tiled=True),
        lax.psum_scatter(bias_stack, ("dp", "tensor"), scatter_dimension=1, tiled=True),
    )
    return (
        loss,
        result.astype(jnp.bfloat16),
        tokens_grad,
        qkv_part,
        out_part,
        up_part,
        down_part,
        gain_part,
        bias_part,
    )


def solution(mesh):
    return jax.shard_map(
        on_device,
        mesh=mesh,
        in_specs=(
            P(("dp", "tensor"), None),
            P(("dp", "tensor"), None),
            P("dp"),
            P("dp", None, "tensor"),
            P("dp", "tensor"),
            P("dp", "tensor"),
            P("dp", "tensor"),
            P(),
            P(),
        ),
        out_specs=(
            P(),
            P(("dp", "tensor"), None),
            P(("dp", "tensor"), None),
            P("dp", None, "tensor"),
            P("dp", "tensor"),
            P("dp", "tensor"),
            P("dp", "tensor"),
            P(None, ("dp", "tensor")),
            P(None, ("dp", "tensor")),
        ),
        check_vma=False,
    )
```

profile of v0, /device:TPU:0, one launch (start us, length us, event | category | flops | bytes accessed | tf_op | source)
XLA Modules:
  0.0 1114.9 jit_solution(10969481836749397410)
XLA Ops:
  12.7 2.1 fusion.39
  17.6 9.2 all-gather.9.cloned.1.call-done
  26.7 71.6 %all-gather.11.cloned.1.call-done = bf16[1024,3,512]{2,0,1:T(8,128)(2,1)} async-done(((bf16[64,3,512]{2,0,1:T(8,128)(2,1)}), bf16[1024,3,512]{2,0,1:T(8,128)(2,1)}) %all-gather.11.cloned.1.call-update) | async-done | bytes 3145744 | tf_op jit(solution)/shard_map/all_gather | solution.py:166
  98.3 4.1 fusion.56
  104.5 1.7 fusion
  107.9 3.2 fusion.91
  111.1 44.3 %all-gather.13.cloned.1.call-done = bf16[1024,512]{1,0:T(8,128)(2,1)} async-done(((bf16[64,512]{1,0:T(8,128)(2,1)}), bf16[1024,512]{1,0:T(8,128)(2,1)}) %all-gather.13.cloned.1.call-update) | async-done | bytes 1048592 | tf_op jit(solution)/shard_map/all_gather | solution.py:167
  155.5 3.0 convolution_convert_fusion.4
  159.1 6.9 reduce-scatter.15.cloned.1.call-done
  170.6 1.5 multiply_reduce_fusion.1
  172.2 2.6 add_convert_fusion.3
  175.9 70.4 %all-gather.17.cloned.1.call-done = bf16[1024,2048]{1,0:T(8,128)(2,1)} async-done(((bf16[64,2048]{1,0:T(8,128)(2,1)}), bf16[1024,2048]{1,0:T(8,128)(2,1)}) %all-gather.17.cloned.1.call-update) | async-done | bytes 4194320 | tf_op jit(solution)/shard_map/all_gather | solution.py:168
  246.3 9.7 all-gather.15.cloned.1.call-done
  256.0 15.0 %multiply_convert_fusion.1 = (bf16[512,2048]{1,0:T(8,128)(2,1)}, f32[512,2048]{1,0:T(8,128)}, f32[512,2048]{1,0:T(8,128)}) fusion(bf16[512,1024]{1,0:T(8,128)(2,1)} %all-gather.15.cloned.1.call-done, bf16[1024,2048]{1,0:T(8,128)(2,1)} %all-gather.17.cloned.1.call-done), kind=kOutput, calls=%fused_computation.10 | convolution fusion | flops 2215641088 | bytes 15728640 | tf_op jit(solution)/shard_map/dot_general | solution.py:186
  271.1 65.4 %all-gather.19.cloned.1.call-done = bf16[1024,2048]{1,0:T(8,128)(2,1)} async-done(((bf16[64,2048]{1,0:T(8,128)(2,1)}), bf16[1024,2048]{1,0:T(8,128)(2,1)}) %all-gather.19.cloned.1.call-update) | async-done | bytes 4194320 | tf_op jit(solution)/shard_map/all_gather | solution.py:169
  336.4 6.3 convolution_convert_fusion.6
  343.4 39.5 %psum.15 = f32[]{:T(128)} all-reduce(f32[]{:T(128)} %fusion.82), channel_id=1, replica_groups=mesh['dp'=16,'tensor'=2] {'dp','tensor'}, use_global_device_ids=true, to_apply=%region_15.16 | all-reduce | flops 1 | bytes 8 | tf_op jit(solution)/shard_map/psum | solution.py:192
  386.7 2.7 fusion.42
  392.0 9.2 all-gather.21.cloned.1.call-done
  401.2 8.5 add_convert_fusion
  411.0 3.4 convolution_convert_fusion.5
  414.6 9.8 reduce-scatter.19.cloned.1.call-done
  424.4 2.4 convert_reduce_fusion.1
  427.5 3.7 fusion.53
  431.2 2.3 fusion.44
  437.3 9.4 all-gather.23.cloned.1.call-done
  446.6 2.5 multiply_reduce_fusion
  449.1 6.1 fusion.27
  455.3 4.4 multiply_convert_fusion
  461.1 1.8 fusion.18
  464.1 1.5 subtract_convert_fusion.1
  467.7 5.1 bitcast_convert_fusion
  472.9 2.8 convolution_convert_fusion.3
  475.8 6.9 reduce-scatter.21.cloned.1.call-done
  484.2 1.6 fusion.54
  488.2 5.9 convolution_convert_fusion.1
  495.3 5.9 convolution_convert_fusion
  502.3 5.0 convolution_convert_fusion.2
  507.9 41.1 %psum.14 = f32[]{:T(128)} all-reduce(f32[]{:T(128)} %get-tuple-element.119), channel_id=1, replica_groups=mesh['dp'=16,'tensor'=2] {'dp','tensor'}, use_global_device_ids=true, to_apply=%region_13.14 | all-reduce | flops 1 | bytes 8 | tf_op jit(solution)/shard_map/psum | solution.py:192
  549.7 14.5 %reduce-scatter.25.cloned.1.call-done = bf16[64,512]{1,0:T(8,128)(2,1)} async-done(((bf16[1024,512]{1,0:T(8,128)(2,1)}), bf16[64,512]{1,0:T(8,128)(2,1)}) %reduce-scatter.25.cloned.1.call-update) | async-done | bytes 65552 | tf_op jit(solution)/shard_map/reduce_scatter | solution.py:248
  567.1 129.3 %reduce-scatter.31.cloned.1.call-done = f32[32,4]{1,0:T(8,128)} async-done(((f32[1024,4]{1,0:T(8,128)}), f32[32,4]{1,0:T(8,128)}) %reduce-scatter.31.cloned.1.call-update) | async-done | bytes 528
  697.8 130.7 %reduce-scatter.33.cloned.1.call-done = f32[32,4]{1,0:T(8,128)} async-done(((f32[1024,4]{1,0:T(8,128)}), f32[32,4]{1,0:T(8,128)}) %reduce-scatter.33.cloned.1.call-update) | async-done | bytes 528
  829.8 92.0 %reduce-scatter.27.cloned.1.call-done = bf16[64,2048]{1,0:T(8,128)(2,1)} async-done(((bf16[1024,2048]{1,0:T(8,128)(2,1)}), bf16[64,2048]{1,0:T(8,128)(2,1)}) %reduce-scatter.27.cloned.1.call-update) | async-done | bytes 262160 | tf_op jit(solution)/shard_map/reduce_scatter | solution.py:251
  921.8 1.8 convert_element_type.231
  923.6 95.2 %reduce-scatter.29.cloned.1.call-done = bf16[64,2048]{1,0:T(8,128)(2,1)} async-done(((bf16[1024,2048]{1,0:T(8,128)(2,1)}), bf16[64,2048]{1,0:T(8,128)(2,1)}) %reduce-scatter.29.cloned.1.call-update) | async-done | bytes 262160 | tf_op jit(solution)/shard_map/reduce_scatter | solution.py:254
  1018.8 1.8 convert_element_type.233
  1020.6 84.4 %reduce-scatter.23.cloned.1.call-done = bf16[64,3,512]{2,0,1:T(8,128)(2,1)} async-done(((bf16[1024,3,512]{2,0,1:T(8,128)(2,1)}), bf16[64,3,512]{2,0,1:T(8,128)(2,1)}) %reduce-scatter.23.cloned.1.call-update) | async-done | bytes 196624 | tf_op jit(solution)/shard_map/reduce_scatter | solution.py:245
  1105.0 1.7 convert_element_type.227
  (190 shorter events, 46.0 us)
Async XLA Ops:
  7.2 19.6 %all-gather.9.cloned.1.call-start = ((), (), s32[]{:S(2)}) async-start(), calls=%async_computation.10 | async-start | bytes 1572864 | tf_op jit(solution)/shard_map/all_gather | solution.py:118
  8.4 8.7 copy-start.24
  9.8 92.6 %copy-start.38 = (f32[256]{0:T(256)}, f32[256]{0:T(256)S(1)}, u32[]{:S(2)}) copy-start(f32[256]{0:T(256)S(1)} %fusion.51) | copy-start | bytes 3076
  9.8 92.6 %copy-start.33 = (f32[256]{0:T(256)}, f32[256]{0:T(256)S(1)}, u32[]{:S(2)}) copy-start(f32[256]{0:T(256)S(1)} %fusion.69) | copy-start | bytes 3076
  11.3 160.9 %copy-start.19 = (f32[1,1024]{1,0:T(1,128)}, f32[1,1024]{1,0:T(1,128)S(1)}, u32[]{:S(2)}) copy-start(f32[1,1024]{1,0:T(1,128)S(1)} %get-tuple-element.158) | copy-start | bytes 12292
  14.9 83.4 %all-gather.11.cloned.1.call-start = ((), (), s32[]{:S(2)}) async-start(), calls=%async_computation.11 | async-start | bytes 3342336 | tf_op jit(solution)/shard_map/all_gather | solution.py:166
  15.6 139.9 %all-gather.13.cloned.1.call-start = ((), (), s32[]{:S(2)}) async-start(), calls=%async_computation.12 | async-start | bytes 1114112 | tf_op jit(solution)/shard_map/all_gather | solution.py:167
  16.3 149.7 %reduce-scatter.15.cloned.1.call-start = ((), (), s32[]{:S(2)}) async-start(), calls=%async_computation.13 | async-start | bytes 1572864 | tf_op jit(solution)/shard_map/reduce_scatter | solution.py:127
  17.2 89.1 %copy-start.16 = (pred[512,512]{0,1:T(8,128)(4,1)}, pred[512,512]{0,1:T(8,128)(4,1)S(1)}, u32[]{:S(2)}) copy-start(pred[512,512]{0,1:T(8,128)(4,1)S(1)} %fusion.58) | copy-start | bytes 786436
  111.1 57.4 %copy-start.45 = (bf16[512,8,64]{0,2,1:T(8,128)(2,1)}, bf16[512,8,64]{0,2,1:T(8,128)(2,1)S(1)}, u32[]{:S(2)}) copy-start(bf16[512,8,64]{0,2,1:T(8,128)(2,1)S(1)} %get-tuple-element.164) | copy-start | bytes 1572868
  111.1 58.0 %copy-start = (bf16[256,1024]{1,0:T(8,128)(2,1)S(1)}, bf16[256,1024]{1,0:T(8,128)(2,1)}, u32[]{:S(2)}) copy-start(bf16[256,1024]{1,0:T(8,128)(2,1)} %param.17) | copy-start | bytes 1572868
  158.5 87.8 %all-gather.17.cloned.1.call-start = ((), (), s32[]{:S(2)}) async-start(), calls=%async_computation.15 | async-start | bytes 4456448 | tf_op jit(solution)/shard_map/all_gather | solution.py:168
  159.1 96.9 %all-gather.15.cloned.1.call-start = ((), (), s32[]{:S(2)}) async-start(), calls=%async_computation.14 | async-start | bytes 1572864 | tf_op jit(solution)/shard_map/all_gather | solution.py:118
  168.6 102.5 %copy-start.21 = (f32[256]{0:T(256)}, f32[256]{0:T(256)S(1)}, u32[]{:S(2)}) copy-start(f32[256]{0:T(256)S(1)} %fusion.70) | copy-start | bytes 3076
  170.6 100.5 %copy-start.26 = (f32[256]{0:T(256)}, f32[256]{0:T(256)S(1)}, u32[]{:S(2)}) copy-start(f32[256]{0:T(256)S(1)} %broadcast_multiply_fusion.1) | copy-start | bytes 3076
  172.1 98.9 %copy-start.41 = (f32[256]{0:T(256)}, f32[256]{0:T(256)S(1)}, u32[]{:S(2)}) copy-start(f32[256]{0:T(256)S(1)} %multiply_reduce_fusion.1) | copy-start | bytes 3076
  172.2 98.9 %copy-start.35 = (f32[256]{0:T(256)}, f32[256]{0:T(256)S(1)}, u32[]{:S(2)}) copy-start(f32[256]{0:T(256)S(1)} %fusion.71) | copy-start | bytes 3076
  174.8 161.6 %all-gather.19.cloned.1.call-start = ((), (), s32[]{:S(2)}) async-start(), calls=%async_computation.16 | async-start | bytes 4456448 | tf_op jit(solution)/shard_map/all_gather | solution.py:169
  175.6 208.5 %reduce-scatter.17.cloned.1.call-start = ((), (), s32[]{:S(2)}) async-start(), calls=%async_computation.17 | async-start | bytes 1572864 | tf_op jit(solution)/shard_map/reduce_scatter | solution.py:127
  336.4 50.3 %copy-start.1 = (bf16[256,1024]{1,0:T(8,128)(2,1)S(1)}, bf16[256,1024]{1,0:T(8,128)(2,1)}, u32[]{:S(2)}) copy-start(bf16[256,1024]{1,0:T(8,128)(2,1)} %reduce-scatter.15.cloned.1.call-done) | copy-start | bytes 1572868
  336.4 50.3 %copy-start.6 = (bf16[256,1024]{1,0:T(8,128)(2,1)S(1)}, bf16[256,1024]{1,0:T(8,128)(2,1)}, u32[]{:S(2)}) copy-start(bf16[256,1024]{1,0:T(8,128)(2,1)} %param.18) | copy-start | bytes 1572868
  342.7 58.5 %all-gather.21.cloned.1.call-start = ((), (), s32[]{:S(2)}) async-start(), calls=%async_computation.18 | async-start | bytes 1572864 | tf_op jit(solution)/shard_map/all_gather | solution.py:122
  391.5 32.8 %reduce-scatter.19.cloned.1.call-start = ((), (), s32[]{:S(2)}) async-start(), calls=%async_computation.19 | async-start | bytes 1572864 | tf_op jit(solution)/shard_map/reduce_scatter | solution.py:139
  401.2 9.8 copy-start.42
  414.5 32.1 %all-gather.23.cloned.1.call-start = ((), (), s32[]{:S(2)}) async-start(), calls=%async_computation.20 | async-start | bytes 1572864 | tf_op jit(solution)/shard_map/all_gather | solution.py:122
  424.4 6.8 copy-start.5
  424.4 6.8 copy-start.20
  433.5 13.2 %copy-start.8 = (bf16[1024,512]{1,0:T(8,128)(2,1)S(1)}, bf16[1024,512]{1,0:T(8,128)(2,1)}, u32[]{:S(2)}) copy-start(bf16[1024,512]{1,0:T(8,128)(2,1)} %all-gather.13.cloned.1.call-done) | copy-start | bytes 3145732
  435.3 13.8 %copy-start.17 = (pred[512,512]{0,1:T(8,128)(4,1)S(1)}, pred[512,512]{0,1:T(8,128)(4,1)}, u32[]{:S(2)}) copy-start(pred[512,512]{0,1:T(8,128)(4,1)} %copy-done.16) | copy-start | bytes 786436
  436.3 46.4 %reduce-scatter.21.cloned.1.call-start = ((), (), s32[]{:S(2)}) async-start(), calls=%async_computation.21 | async-start | bytes 1572864 | tf_op jit(solution)/shard_map/reduce_scatter | solution.py:139
  446.6 8.6 slice-start
  472.8 9.9 copy-start.25
  472.8 11.4 %copy-start.39 = (f32[256]{0:T(256)S(1)}, f32[256]{0:T(256)}, u32[]{:S(2)}) copy-start(f32[256]{0:T(256)} %copy-done.38) | copy-start | bytes 3076
  472.8 11.4 %copy-start.34 = (f32[256]{0:T(256)S(1)}, f32[256]{0:T(256)}, u32[]{:S(2)}) copy-start(f32[256]{0:T(256)} %copy-done.33) | copy-start | bytes 3076
  472.8 13.0 %copy-start.30 = (f32[1024]{0:T(1024)S(1)}, f32[1024]{0:T(1024)}, u32[]{:S(2)}) copy-start(f32[1024]{0:T(1024)} %get-tuple-element.117) | copy-start | bytes 12292
  472.8 13.1 %copy-start.32 = (f32[1024]{0:T(1024)S(1)}, f32[1024]{0:T(1024)}, u32[]{:S(2)}) copy-start(f32[1024]{0:T(1024)} %get-tuple-element.113) | copy-start | bytes 12292
  472.8 13.1 %copy-start.37 = (f32[1024]{0:T(1024)S(1)}, f32[1024]{0:T(1024)}, u32[]{:S(2)}) copy-start(f32[1024]{0:T(1024)} %get-tuple-element.115) | copy-start | bytes 12292
  472.8 14.2 %copy-start.29 = (f32[1024]{0:T(1024)S(1)}, f32[1024]{0:T(1024)}, u32[]{:S(2)}) copy-start(f32[1024]{0:T(1024)} %get-tuple-element.123) | copy-start | bytes 12292
  472.8 14.2 %copy-start.31 = (f32[1024]{0:T(1024)S(1)}, f32[1024]{0:T(1024)}, u32[]{:S(2)}) copy-start(f32[1024]{0:T(1024)} %get-tuple-element.126) | copy-start | bytes 12292
  472.8 14.2 %copy-start.36 = (f32[1024]{0:T(1024)S(1)}, f32[1024]{0:T(1024)}, u32[]{:S(2)}) copy-start(f32[1024]{0:T(1024)} %get-tuple-element.122) | copy-start | bytes 12292
  472.9 91.3 %reduce-scatter.25.cloned.1.call-start = ((), (), s32[]{:S(2)}) async-start(), calls=%async_computation.23 | async-start | bytes 1114112 | tf_op jit(solution)/shard_map/reduce_scatter | solution.py:248
  475.7 12.5 %copy-start.43 = (bf16[512,1024]{1,0:T(8,128)(2,1)S(1)}, bf16[512,1024]{1,0:T(8,128)(2,1)}, u32[]{:S(2)}) copy-start(bf16[512,1024]{1,0:T(8,128)(2,1)} %all-gather.15.cloned.1.call-done) | copy-start | bytes 3145732
  475.7 220.7 %reduce-scatter.31.cloned.1.call-start = ((), (), s32[]{:S(2)}) async-start(), calls=%async_computation.26 | async-start | bytes 540672
  487.0 341.5 %reduce-scatter.33.cloned.1.call-start = ((), (), s32[]{:S(2)}) async-start(), calls=%async_computation.27 | async-start | bytes 540672
  488.1 433.6 %reduce-scatter.27.cloned.1.call-start = ((), (), s32[]{:S(2)}) async-start(), calls=%async_computation.24 | async-start | bytes 4456448 | tf_op jit(solution)/shard_map/reduce_scatter | solution.py:251
  494.1 524.6 %reduce-scatter.29.cloned.1.call-start = ((), (), s32[]{:S(2)}) async-start(), calls=%async_computation.25 | async-start | bytes 4456448 | tf_op jit(solution)/shard_map/reduce_scatter | solution.py:254
  501.3 64.4 %copy-start.4 = (bf16[256,1024]{1,0:T(8,128)(2,1)S(1)}, bf16[256,1024]{1,0:T(8,128)(2,1)}, u32[]{:S(2)}) copy-start(bf16[256,1024]{1,0:T(8,128)(2,1)} %reduce-scatter.21.cloned.1.call-done) | copy-start | bytes 1572868
  501.3 603.7 %reduce-scatter.23.cloned.1.call-start = ((), (), s32[]{:S(2)}) async-start(), calls=%async_computation.22 | async-start | bytes 3342336 | tf_op jit(solution)/shard_map/reduce_scatter | solution.py:245
  (19 other events, 57.4 us)
Sparse Core Ops, SparseCore 0:
  15.0 11.7 all-gather.8
  29.5 68.7 all-gather.10
  101.1 54.3 all-gather.12
  158.6 7.3 reduce-scatter.14
  169.0 77.2 all-gather.16
  248.3 7.6 all-gather.14
  259.1 77.2 all-gather.18
  342.8 7.1 reduce-scatter.16
  391.6 9.5 all-gather.20
  414.6 9.6 reduce-scatter.18
  436.4 10.1 all-gather.22
  473.0 9.6 reduce-scatter.20
  485.0 79.1 reduce-scatter.24
  566.4 129.9 reduce-scatter.30
  698.5 129.9 reduce-scatter.32
  830.7 91.0 reduce-scatter.26
  924.0 94.7 reduce-scatter.28
  1021.0 83.8 reduce-scatter.22
where the time goes:
time: 1120 us; the launch traced here: 1110 us
  waiting for transfers between devices  862 us (77%)
  matrix products  85.8 us (8%)
  blocking collectives  80.6 us (7%)
  other arithmetic  49.4 us (4%)
  between operations  18.9 us (2%)
  local copies, waits for them, and re-layouts  16.7 us (1%)
    unnamed x20, waiting for transfers between devices  263 us
    reduce_scatter x1, waiting for transfers between devices, on_device(): lax.psum_scatter(down_grad.astype(jnp.bfloat16), 'dp', scatter_dimension=...  95.2 us
    reduce_scatter x1, waiting for transfers between devices, on_device(): lax.psum_scatter(up_grad.astype(jnp.bfloat16), 'dp', scatter_dimension=0,...  92 us
    reduce_scatter x1, waiting for transfers between devices, on_device(): lax.psum_scatter(qkv_grad.astype(jnp.bfloat16), 'dp', scatter_dimension=0...  84.4 us
    psum x2, blocking collectives, on_device(): squared, count = lax.psum((own_squared, jnp.sum(valid)), ('dp', 'tensor'))  80.6 us
    all_gather x1, waiting for transfers between devices, on_device(): lax.all_gather(w_qkv, 'dp', axis=0, tiled=True)  71.6 us
    all_gather x1, waiting for transfers between devices, on_device(): lax.all_gather(w_up, 'dp', axis=0, tiled=True)  70.4 us
    all_gather x1, waiting for transfers between devices, on_device(): lax.all_gather(w_down, 'dp', axis=0, tiled=True)  65.4 us
  transfers between devices with their start and end apart: 18, of which 17 were waited for; matrix products, arithmetic and copies ran while one was open for 6% of the time, Pallas kernels for 0%

commit v1 on v0

v1 whole, which is shorter than its diff:
```python
import jax
import jax.numpy as jnp
from jax import lax
from jax.sharding import PartitionSpec as P

HEAD_DIM = 64


norm_eps = 1e-05


def norm_stats(values):
    center = values - jnp.mean(values, axis=-1, keepdims=True)
    spread = jnp.mean(center * center, axis=-1, keepdims=True)
    inv = lax.rsqrt(spread + norm_eps)
    return center * inv, inv


def norm_back(grad, normal, inv, gain):
    e = grad * gain
    back = inv * (
        e
        - jnp.mean(e, axis=-1, keepdims=True)
        - normal * jnp.mean(e * normal, axis=-1, keepdims=True)
    )
    return back, jnp.sum(grad * normal, axis=0), jnp.sum(grad, axis=0)


def rotary_tables(slot_count, head_size):
    places = jnp.arange(slot_count).astype(jnp.float32)
    freqs = 10000.0 ** (-2.0 * jnp.arange(head_size // 2).astype(jnp.float32) / head_size)
    angles = places[:, None] * freqs[None, :]
    return (jnp.cos(angles)[:, None, :], jnp.sin(angles)[:, None, :])


def rotate_pairs(values, cosine, sine):
    half_size = values.shape[-1] // 2
    front = values[..., :half_size]
    back_half = values[..., half_size:]
    return jnp.concatenate(
        [front * cosine - back_half * sine, back_half * cosine + front * sine], axis=-1
    )


def allowed_pairs(begin, block, key_count, length):
    key_places = jnp.arange(key_count)
    query_places = begin + jnp.arange(block)
    return (key_places[None, :] <= query_places[:, None]) & (key_places[None, :] < length)


def attend_forward(packed):
    queries, key_rows, value_rows, length = packed
    slot_count = queries.shape[0]
    block = min(512, slot_count)
    scale = HEAD_DIM ** (-0.5)
    outputs = []
    totals = []
    for begin in range(0, slot_count, block):
        finish = begin + block
        scores = (
            jnp.einsum(
                "qhd,khd->hqk",
                queries[begin:finish],
                key_rows[:finish],
                preferred_element_type=jnp.float32,
            )
            * scale
        )
        allowed = allowed_pairs(begin, block, finish, length)
        scores = jnp.where(allowed[None], scores, -1000000000.0)
        top_score = jnp.max(scores, axis=-1, keepdims=True)
        weights = jnp.exp(scores - top_score)
        weight_sum = jnp.sum(weights, axis=-1, keepdims=True)
        probs = (weights / weight_sum).astype(jnp.bfloat16)
        outputs.append(
            jnp.einsum(
                "hqk,khd->qhd", probs, value_rows[:finish], preferred_element_type=jnp.float32
            )
        )
        totals.append((top_score + jnp.log(weight_sum))[:, :, 0])
    return (jnp.concatenate(outputs, axis=0), jnp.concatenate(totals, axis=1))


def attend_backward(packed):
    queries, key_rows, value_rows, outputs, out_grads, totals, length = packed
    slot_count = queries.shape[0]
    block = min(512, slot_count)
    scale = HEAD_DIM ** (-0.5)
    delta = jnp.sum(out_grads.astype(jnp.float32) * outputs, axis=-1).T
    key_grads = jnp.zeros(key_rows.shape, jnp.float32)
    value_grads = jnp.zeros(value_rows.shape, jnp.float32)
    query_grads = []
    for begin in range(0, slot_count, block):
        finish = begin + block
        query_block = queries[begin:finish]
        grad_block = out_grads[begin:finish]
        key_part = key_rows[:finish]
        value_part = value_rows[:finish]
        scores = (
            jnp.einsum("qhd,khd->hqk", query_block, key_part, preferred_element_type=jnp.float32)
            * scale
        )
        allowed = allowed_pairs(begin, block, finish, length)
        probs = jnp.where(allowed[None], jnp.exp(scores - totals[:, begin:finish, None]), 0.0)
        value_grads = value_grads.at[:finish].add(
            jnp.einsum(
                "hqk,qhd->khd",
                probs.astype(jnp.bfloat16),
                grad_block,
                preferred_element_type=jnp.float32,
            )
        )
        prob_grads = jnp.einsum(
            "qhd,khd->hqk", grad_block, value_part, preferred_element_type=jnp.float32
        )
        score_grads = (probs * (prob_grads - delta[:, begin:finish, None])).astype(jnp.bfloat16)
        query_grads.append(
            jnp.einsum("hqk,khd->qhd", score_grads, key_part, preferred_element_type=jnp.float32)
            * scale
        )
        key_grads = key_grads.at[:finish].add(
            jnp.einsum("hqk,qhd->khd", score_grads, query_block, preferred_element_type=jnp.float32)
            * scale
        )
    return (jnp.concatenate(query_grads, axis=0), key_grads, value_grads)


def swap(values, bit):
    size = lax.axis_size("dp")
    return lax.ppermute(values, "dp", [(j, j ^ (1 << bit)) for j in range(size)])


def swap_core(values):
    return lax.ppermute(values, "tensor", [(0, 1), (1, 0)])


def add_low(*terms):
    total = terms[0].astype(jnp.float32)
    for term in terms[1:]:
        total = total + term.astype(jnp.float32)
    return total


def low(values):
    return values.astype(jnp.bfloat16)


def bit_order(members):
    bits = members.bit_length() - 1
    return (1, 0) + tuple(range(bits - 1, 1, -1))


def relative_map(members, width):
    order = bit_order(members)
    block = width // members
    rel = jnp.arange(width)
    place = rel // block
    mask = jnp.zeros_like(rel)
    for k, bit in enumerate(order):
        mask = mask | (((place >> (len(order) - 1 - k)) & 1) << bit)
    source = (lax.axis_index("dp") ^ mask) * block + rel % block
    return (jnp.arange(width)[:, None] == source[None, :]).astype(jnp.bfloat16)


def gather_rows(part):
    bits = lax.axis_size("dp").bit_length() - 1
    own = part
    for bit in range(2, bits):
        own = jnp.concatenate([own, swap(own, bit)], axis=0)
    half = own.shape[1] // 2
    over_x = swap(own, 0)
    over_y = swap(own, 1)
    corner = jnp.concatenate([swap(over_x[:, :half], 1), swap(over_y[:, half:], 0)], axis=1)
    return jnp.concatenate([own, over_x, over_y, corner], axis=0)


def scatter_rows(blocks):
    here, over_x, over_y, corner = blocks
    bits = lax.axis_size("dp").bit_length() - 1
    half = here.shape[1] // 2
    from_y = swap(corner[:, :half], 1)
    from_x = swap(corner[:, half:], 0)
    to_x = jnp.concatenate([low(add_low(over_x[:, :half], from_y)), over_x[:, half:]], axis=1)
    to_y = jnp.concatenate([over_y[:, :half], low(add_low(over_y[:, half:], from_x))], axis=1)
    got_x = swap(to_x, 0)
    got_y = swap(to_y, 1)
    terms = [here, got_x, got_y]
    for bit in range(bits - 1, 1, -1):
        cut = terms[0].shape[0] // 2
        got = swap(low(add_low(*[t[cut:] for t in terms])), bit)
        terms = [low(add_low(*[t[:cut] for t in terms])), got]
    return add_low(*terms)


def grad_blocks(left, right):
    step = left.shape[1] // 4
    outs = [
        low(
            lax.dot_general(
                left[:, k * step : (k + 1) * step],
                right,
                (((0,), (0,)), ((), ())),
                preferred_element_type=jnp.float32,
            )
        )
        for k in (3, 1, 2, 0)
    ]
    return outs[3], outs[1], outs[2], outs[0]


def collect_rows(values):
    groups = lax.axis_size("tensor")
    if groups != 2:
        return lax.all_gather(values, "tensor", axis=0, tiled=True)
    other = swap_core(values)
    first = lax.axis_index("tensor") == 0
    return jnp.concatenate(
        [jnp.where(first, values, other), jnp.where(first, other, values)], axis=0
    )


def product_reduce(inputs, weight, dims, own_rows):
    groups = lax.axis_size("tensor")

    def product(rows):
        return low(lax.dot_general(rows, weight, dims, preferred_element_type=jnp.float32))

    if groups != 2:
        return lax.psum_scatter(
            product(inputs), "tensor", scatter_dimension=0, tiled=True
        ).astype(jnp.float32)
    me = lax.axis_index("tensor")
    away = product(lax.dynamic_slice_in_dim(inputs, (1 - me) * own_rows, own_rows, 0))
    got = swap_core(away)
    mine = product(lax.dynamic_slice_in_dim(inputs, me * own_rows, own_rows, 0))
    return add_low(mine, got)


def on_device(tokens, teacher, lengths, w_qkv, w_out, w_up, w_down, norm_gain, norm_bias):
    tok_dev, width = tokens.shape
    groups = lax.axis_size("tensor")
    members = lax.axis_size("dp")
    bits = members.bit_length() - 1
    row_count = lengths.shape[0]
    group_tokens = tok_dev * groups
    slot_count = group_tokens // row_count
    all_slots = group_tokens * members
    me = lax.axis_index("tensor")
    places = me * tok_dev + jnp.arange(tok_dev)
    row_index = places // slot_count
    row_length = jnp.sum(
        jnp.where(row_index[:, None] == jnp.arange(row_count)[None, :], lengths[None, :], 0), axis=1
    )
    valid = (places % slot_count < row_length).astype(jnp.float32)[:, None]
    cosine, sine = rotary_tables(slot_count, HEAD_DIM)
    local_width = w_qkv.shape[2]
    heads_here = local_width // HEAD_DIM
    out_width = w_out.shape[1]
    hidden_width = w_up.shape[1]

    weight_qkv = gather_rows(w_qkv.reshape(w_qkv.shape[0], 3 * local_width))
    joined = gather_rows(jnp.concatenate([w_out, w_up], axis=1))
    weight_out, weight_up = joined[:, :out_width], joined[:, out_width:]
    weight_down = gather_rows(w_down)

    count = jnp.sum(lengths).astype(jnp.float32).reshape(1, 1)
    for bit in range(bits):
        count = count + swap(count, bit)

    to_rel = relative_map(members, width)

    def relative(values):
        return jnp.dot(values, to_rel, preferred_element_type=jnp.float32)

    def absolute(values, precision=None):
        return lax.dot_general(
            values,
            to_rel.astype(values.dtype),
            (((1,), (1,)), ((), ())),
            precision=precision,
            preferred_element_type=jnp.float32,
        )

    inputs = relative(tokens)
    target = relative(teacher)
    affine = jnp.dot(
        jnp.concatenate([norm_gain, norm_bias], axis=0),
        to_rel.astype(jnp.float32),
        precision=lax.Precision.HIGHEST,
        preferred_element_type=jnp.float32,
    )
    gain, bias = affine[:4], affine[4:]

    normal_zero, inv_zero = norm_stats(inputs)
    rows_one = collect_rows(low(normal_zero * gain[0] + bias[0]))
    mixed = jnp.dot(rows_one, weight_qkv, preferred_element_type=jnp.float32)
    mixed = mixed.reshape(row_count, slot_count, 3, heads_here, HEAD_DIM)
    queries = low(rotate_pairs(mixed[:, :, 0], cosine, sine))
    key_rows = low(rotate_pairs(mixed[:, :, 1], cosine, sine))
    value_rows = low(mixed[:, :, 2])
    attended, totals = lax.map(attend_forward, (queries, key_rows, value_rows, lengths))
    attended_low = low(attended.reshape(group_tokens, local_width))
    across = (((1,), (1,)), ((), ()))
    attn_sum = product_reduce(attended_low, weight_out, across, tok_dev)
    normal_one, inv_one = norm_stats(attn_sum)
    middle = inputs + normal_one * gain[1] + bias[1]
    normal_two, inv_two = norm_stats(middle)
    rows_two = collect_rows(low(normal_two * gain[2] + bias[2]))
    hidden = jnp.dot(rows_two, weight_up, preferred_element_type=jnp.float32)
    gate = 0.5 * (1.0 + lax.erf(hidden * (2.0**-0.5)))
    active = low(hidden * gate)
    slope = low(gate + hidden * jnp.exp(-0.5 * hidden * hidden) * ((2.0 * jnp.pi) ** -0.5))
    mlp_sum = product_reduce(active, weight_down, across, tok_dev)
    normal_three, inv_three = norm_stats(mlp_sum)
    result = middle + normal_three * gain[3] + bias[3]
    error = result - target
    squared = jnp.sum(valid * error * error)
    out_grad = valid * error * (all_slots / count)

    mlp_grad, gain_three, bias_three = norm_back(out_grad, normal_three, inv_three, gain[3])
    mlp_rows = collect_rows(low(mlp_grad))
    down_part = scatter_rows(grad_blocks(mlp_rows, active))
    active_grad = jnp.dot(mlp_rows, weight_down, preferred_element_type=jnp.float32)
    hidden_grad = low(active_grad * slope.astype(jnp.float32))
    up_part = scatter_rows(grad_blocks(rows_two, hidden_grad))
    normed_two_grad = product_reduce(hidden_grad, weight_up, across, tok_dev)
    middle_extra, gain_two, bias_two = norm_back(normed_two_grad, normal_two, inv_two, gain[2])
    middle_grad = out_grad + middle_extra
    attn_grad, gain_one, bias_one = norm_back(middle_grad, normal_one, inv_one, gain[1])
    attn_rows = collect_rows(low(attn_grad))
    attended_grad = low(jnp.dot(attn_rows, weight_out, preferred_element_type=jnp.float32))
    out_part = scatter_rows(grad_blocks(attn_rows, attended_low))
    attended_grad = attended_grad.reshape(row_count, slot_count, heads_here, HEAD_DIM)
    query_grads, key_grads, value_grads = lax.map(
        attend_backward, (queries, key_rows, value_rows, attended, attended_grad, totals, lengths)
    )
    mixed_grad = jnp.stack(
        [
            rotate_pairs(query_grads, cosine, -sine),
            rotate_pairs(key_grads, cosine, -sine),
            value_grads,
        ],
        axis=2,
    )
    mixed_grad = low(mixed_grad.reshape(group_tokens, 3 * local_width))
    qkv_part = scatter_rows(grad_blocks(rows_one, mixed_grad))
    normed_one_grad = product_reduce(mixed_grad, weight_qkv, across, tok_dev)
    input_extra, gain_zero, bias_zero = norm_back(normed_one_grad, normal_zero, inv_zero, gain[0])
    tokens_grad = absolute(middle_grad + input_extra, lax.Precision.HIGHEST)

    sums = jnp.stack(
        [
            gain_zero, gain_one, gain_two, gain_three,
            bias_zero, bias_one, bias_two, bias_three,
        ],
        axis=0,
    )
    total = jnp.broadcast_to(squared, (8, 128))
    if groups == 2:
        got = swap_core(jnp.concatenate([sums, total], axis=1))
        sums, total = sums + got[:, :width], total + got[:, width:]
    else:
        sums, total = lax.psum((sums, total), "tensor")
    for bit in bit_order(members):
        cut = sums.shape[1] // 2
        got = swap(jnp.concatenate([sums[:, cut:], total], axis=1), bit)
        sums, total = sums[:, :cut] + got[:, :cut], total + got[:, cut:]
    loss = total[0, 0] / (count[0, 0] * width)
    own = sums.shape[1] // groups
    sums = lax.dynamic_slice_in_dim(sums, me * own, own, 1)
    return (
        loss,
        low(absolute(low(result))),
        tokens_grad,
        qkv_part.reshape(w_qkv.shape),
        out_part,
        up_part,
        down_part,
        sums[:4],
        sums[4:],
    )


def solution(mesh):
    return jax.shard_map(
        on_device,
        mesh=mesh,
        in_specs=(
            P(("dp", "tensor"), None),
            P(("dp", "tensor"), None),
            P("dp"),
            P("dp", None, "tensor"),
            P("dp", "tensor"),
            P("dp", "tensor"),
            P("dp", "tensor"),
            P(),
            P(),
        ),
        out_specs=(
            P(),
            P(("dp", "tensor"), None),
            P(("dp", "tensor"), None),
            P("dp", None, "tensor"),
            P("dp", "tensor"),
            P("dp", "tensor"),
            P("dp", "tensor"),
            P(None, ("dp", "tensor")),
            P(None, ("dp", "tensor")),
        ),
        check_vma=False,
    )
```

time: 1120 us -> 450 us (0.40)
  waiting for transfers between devices: 862 us -> 232 us
  blocking collectives: 80.6 us -> 0 us
  starting transfers between devices: 1.74 us -> 64.6 us
  other arithmetic: 49.4 us -> 31 us
    reduce_scatter x8 -> x0, waiting for transfers between devices: 310 us -> none  [the longest x1 95.2 us: on_device(): lax.psum_scatter(down_grad.astype(jnp.bfloat16), 'dp', scatter_dimension=...]
    all_gather x8 -> x0, waiting for transfers between devices: 289 us -> none  [the longest x1 71.6 us: on_device(): lax.all_gather(w_qkv, 'dp', axis=0, tiled=True)]
    unnamed x20 -> x0, waiting for transfers between devices: 263 us -> none
    ppermute x0 -> x59, waiting for transfers between devices: none -> 232 us  [the longest x50 232 us: swap(): return lax.ppermute(values, 'dp', [(j, j ^ 1 << bit) for j in range(size)])]
    psum x2 -> x0, blocking collectives: 80.6 us -> none  [on_device(): squared, count = lax.psum((own_squared, jnp.sum(valid)), ('dp', 'tensor'))]
    ppermute x0 -> x59, starting transfers between devices: none -> 64.6 us  [the longest x50 63.9 us: swap(): return lax.ppermute(values, 'dp', [(j, j ^ 1 << bit) for j in range(size)])]
    reduce_sum x17 -> x6, other arithmetic: 27.6 us -> 3.46 us  [the longest x1 1.51 us: norm_back(): return (back, jnp.sum(grad * normal, axis=0), jnp.sum(grad, axis=0))]
    dot_general x9 -> x30, matrix products: 41.5 us -> 44.8 us  [the longest x8 15.5 us: product(): lax.dot_general(rows, weight, dims, preferred_element_type=jnp.float32)]
  transfers between devices with their start and end apart: 18 -> 59, of which waited for: 17 -> 30; matrix products, arithmetic and copies ran while one was open for 6% -> 21% of each run, Pallas kernels for 0% -> 0%
where the time goes in v1:
time: 450 us; the launch traced here: 441 us
  waiting for transfers between devices  232 us (52%)
  matrix products  79.1 us (18%)
  starting transfers between devices  64.6 us (14%)
  other arithmetic  31 us (7%)
  local copies, waits for them, and re-layouts  26.1 us (6%)
  between operations  7.81 us (2%)
    ppermute x50, waiting for transfers between devices, swap(): return lax.ppermute(values, 'dp', [(j, j ^ 1 << bit) for j in range(size)])  232 us
    ppermute x50, starting transfers between devices, swap(): return lax.ppermute(values, 'dp', [(j, j ^ 1 << bit) for j in range(size)])  63.9 us
    unnamed x175, local copies, waits for them, and re-layouts  16.9 us
    dot_general x1, matrix products, on_device(): jnp.dot(mlp_rows, weight_down, preferred_element_type=jnp.float32)  15.8 us
    dot_general x8, matrix products, product(): lax.dot_general(rows, weight, dims, preferred_element_type=jnp.float32)  15.5 us
    dot_general x16, matrix products, grad_blocks(): lax.dot_general(left[:, k * step:(k + 1) * step], right, (((0,), (0,)), (...  12.3 us
  transfers between devices with their start and end apart: 59, of which 30 were waited for; matrix products, arithmetic and copies ran while one was open for 21% of the time, Pallas kernels for 0%

profile of v1, /device:TPU:0, one launch (start us, length us, event | category | flops | bytes accessed | tf_op | source)
XLA Modules:
  0.0 440.9 jit_solution(9902522620406586276)
XLA Ops:
  1.7 3.1 collective-permute-start.1
  4.8 2.1 fusion.9
  18.0 2.7 collective-permute-start.2
  23.6 2.0 collective-permute-done.7
  28.6 36.0 %collective-permute-done.2 = bf16[128,1536]{1,0:T(8,128)(2,1)S(1)} collective-permute-done((bf16[128,1536]{1,0:T(8,128)(2,1)S(1)}, bf16[128,1536]{1,0:T(8,128)(2,1)S(1)}, u32[]{:S(2)}, u32[]{:S(2)}) %collective-permute-start.2) | collective-permute-done | bytes 393248 | tf_op jit(solution)/shard_map/ppermute | solution.py:130
  67.8 8.1 %collective-permute-done.16 = bf16[128,2048]{1,0:T(8,128)(2,1)S(1)} collective-permute-done((bf16[128,2048]{1,0:T(8,128)(2,1)S(1)}, bf16[128,2048]{1,0:T(8,128)(2,1)S(1)}, u32[]{:S(2)}, u32[]{:S(2)}) %collective-permute-start.16) | collective-permute-done | bytes 524320 | tf_op jit(solution)/shard_map/ppermute | solution.py:130
  80.0 9.2 %collective-permute-done.8 = bf16[128,2560]{1,0:T(8,128)(2,1)S(1)} collective-permute-done((bf16[128,2560]{1,0:T(8,128)(2,1)S(1)}, bf16[128,2560]{1,0:T(8,128)(2,1)S(1)}, u32[]{:S(2)}, u32[]{:S(2)}) %collective-permute-start.8) | collective-permute-done | bytes 655392 | tf_op jit(solution)/shard_map/ppermute | solution.py:130
  93.3 21.8 %collective-permute-done.6 = bf16[256,768]{1,0:T(8,128)(2,1)S(1)} collective-permute-done((bf16[256,768]{1,0:T(8,128)(2,1)S(1)}, bf16[256,768]{1,0:T(8,128)(2,1)S(1)}, u32[]{:S(2)}, u32[]{:S(2)}) %collective-permute-start.6) | collective-permute-done | bytes 393248 | tf_op jit(solution)/shard_map/ppermute | solution.py:130
  116.6 25.4 %collective-permute-done.5 = bf16[256,768]{1,0:T(8,128)(2,1)S(1)} collective-permute-done((bf16[256,768]{1,0:T(8,128)(2,1)S(1)}, bf16[256,768]{1,0:T(8,128)(2,1)S(1)}, u32[]{:S(2)}, u32[]{:S(2)}) %collective-permute-start.5) | collective-permute-done | bytes 393248 | tf_op jit(solution)/shard_map/ppermute | solution.py:130
  149.3 3.5 fusion.208
  156.3 11.1 %collective-permute-done.12 = bf16[256,1280]{1,0:T(8,128)(2,1)S(1)} collective-permute-done((bf16[256,1280]{1,0:T(8,128)(2,1)S(1)}, bf16[256,1280]{1,0:T(8,128)(2,1)S(1)}, u32[]{:S(2)}, u32[]{:S(2)}) %collective-permute-start.12) | collective-permute-done | bytes 655392 | tf_op jit(solution)/shard_map/ppermute | solution.py:130
  168.8 2.4 copy-done.36
  184.5 3.4 collective-permute-done.20
  189.9 4.1 multiply_convert_fusion.2
  194.0 2.1 convolution_convert_fusion.17
  196.1 2.8 collective-permute-start.22
  200.3 2.9 collective-permute-start.23
  206.0 2.3 collective-permute-done.24
  209.0 2.4 collective-permute-start.25
  211.3 2.2 collective-permute-done.25
  214.3 3.7 fusion.210
  218.3 2.4 multiply_reduce_fusion.1
  222.5 3.7 fusion.44
  227.7 15.8 %multiply_convert_fusion.1 = bf16[512,2048]{1,0:T(8,128)(2,1)S(1)} fusion(bf16[1024,2048]{1,0:T(8,128)(2,1)S(1)} %copy-done.55, f32[512,2048]{1,0:T(8,128)} %get-tuple-element.229, bf16[256,1024]{0,1:T(8,128)(2,1)S(1)} %get-tuple-element.174, bf16[256,1024]{0,1:T(8,128)(2,1)S(1)} %get-tuple-element.173), kind=kOutput, calls=%fused_computation.13 | convolution fusion | flops 2162163712 | bytes 11534336 | tf_op jit(solution)/shard_map/dot_general | solution.py:323
  257.7 2.2 multiply_reduce_fusion.2
  261.9 14.5 %collective-permute-done.55 = bf16[256,1024]{1,0:T(8,128)(2,1)S(1)} collective-permute-done((bf16[256,1024]{1,0:T(8,128)(2,1)S(1)}, bf16[256,1024]{1,0:T(8,128)(2,1)S(1)}, u32[]{:S(2)}, u32[]{:S(2)}) %collective-permute-start.55) | collective-permute-done | bytes 524320 | tf_op jit(solution)/shard_map/ppermute | solution.py:130
  288.0 4.6 %multiply_convert_fusion = bf16[8,512,512]{1,2,0:T(8,128)(2,1)S(1)} fusion(f32[8,512,512]{1,2,0:T(8,128)S(1)} %bitcast.137, f32[8,512]{1,0:T(8,128)S(1)} %bitcast.182, f32[8,512]{1,0:T(8,128)S(1)} %log_add_fusion, pred[512,512]{0,1:T(8,128)(4,1)S(1)} %copy-done.32, bf16[512,8,64]{0,2,1:T(8,128)(2,1)S(1)} %bitcast.181, f32[1,512,3,8,64]{1,4,3,2,0:T(8,128)} %bitcast.144), kind=kOutput, calls=%fused_computation | convolution fusion | flops 281018368 | bytes 13926400 | tf_op jit(solution)/shard_map/while/body/eval_jaxpr/qhd,khd->hqk/dot_general | solution.py:113
  304.0 2.5 collective-permute-done.41
  308.8 7.0 %collective-permute-done.35 = bf16[256,768]{1,0:T(8,128)(2,1)S(1)} collective-permute-done((bf16[256,768]{1,0:T(8,128)(2,1)S(1)}, bf16[256,768]{1,0:T(8,128)(2,1)S(1)}, u32[]{:S(2)}, u32[]{:S(2)}) %collective-permute-start.35) | collective-permute-done | bytes 393248 | tf_op jit(solution)/shard_map/ppermute | solution.py:130
  318.9 4.3 collective-permute-done.44
  323.2 2.2 collective-permute-start.50
  328.5 2.1 multiply_reduce_fusion
  331.4 3.2 collective-permute-done.45
  336.7 2.4 add_convert_fusion.1
  339.1 10.6 %collective-permute-done.50 = bf16[256,2048]{1,0:T(8,128)(2,1)} collective-permute-done((bf16[256,2048]{1,0:T(8,128)(2,1)}, bf16[256,2048]{1,0:T(8,128)(2,1)}, u32[]{:S(2)}, u32[]{:S(2)}) %collective-permute-start.50) | collective-permute-done | bytes 1048608 | tf_op jit(solution)/shard_map/ppermute | solution.py:130
  349.7 2.3 collective-permute-done.48
  352.0 2.0 add_convert_fusion.5
  354.8 7.1 %collective-permute-done.31 = f32[8,640]{1,0:T(8,128)S(1)} collective-permute-done((f32[8,640]{1,0:T(8,128)S(1)}, f32[8,640]{1,0:T(8,128)S(1)}, u32[]{:S(2)}, u32[]{:S(2)}) %collective-permute-start.31) | collective-permute-done | bytes 20512 | tf_op jit(solution)/shard_map/ppermute | solution.py:130
  367.4 5.0 %fusion.8 = f32[256,1024]{1,0:T(8,128)} fusion(s32[1024]{0:T(1024)S(1)} %copy-done.72, f32[256,1024]{0,1:T(8,128)S(1)} %get-tuple-element.148, f32[256,1024]{0,1:T(8,128)S(1)} %copy-done.73, f32[1024,256]{1,0:T(8,128)S(1)} %copy-done.8, f32[256]{0:T(256)S(1)} %broadcast_multiply_fusion, f32[256]{0:T(256)S(1)} %broadcast_multiply_fusion.1, ...), kind=kOutput, calls=%fused_computation.18 | convolution fusion | flops 3224371200 | bytes 4206592 | tf_op jit(solution)/shard_map/dot_general | solution.py:276
  372.4 13.6 %collective-permute-done.33 = f32[8,256]{1,0:T(8,128)S(1)} collective-permute-done((f32[8,256]{1,0:T(8,128)S(1)}, f32[8,256]{1,0:T(8,128)S(1)}, u32[]{:S(2)}, u32[]{:S(2)}) %collective-permute-start.33) | collective-permute-done | bytes 8224 | tf_op jit(solution)/shard_map/ppermute | solution.py:130
  386.2 2.6 collective-permute-start.34
  389.5 8.4 %collective-permute-done.34 = f32[8,192]{1,0:T(8,128)S(1)} collective-permute-done((f32[8,192]{1,0:T(8,128)S(1)}, f32[8,192]{1,0:T(8,128)S(1)}, u32[]{:S(2)}, u32[]{:S(2)}) %collective-permute-start.34) | collective-permute-done | bytes 6176 | tf_op jit(solution)/shard_map/ppermute | solution.py:130
  399.9 2.5 collective-permute-start.58
  402.4 9.1 %collective-permute-done.51 = bf16[128,2048]{1,0:T(8,128)(2,1)S(1)} collective-permute-done((bf16[128,2048]{1,0:T(8,128)(2,1)S(1)}, bf16[128,2048]{1,0:T(8,128)(2,1)S(1)}, u32[]{:S(2)}, u32[]{:S(2)}) %collective-permute-start.51) | collective-permute-done | bytes 524320 | tf_op jit(solution)/shard_map/ppermute | solution.py:130
  412.0 2.3 collective-permute-start.39
  414.4 7.1 %collective-permute-done.58 = bf16[64,2048]{1,0:T(8,128)(2,1)S(1)} collective-permute-done((bf16[64,2048]{1,0:T(8,128)(2,1)S(1)}, bf16[64,2048]{1,0:T(8,128)(2,1)S(1)}, u32[]{:S(2)}, u32[]{:S(2)}) %collective-permute-start.58) | collective-permute-done | bytes 262176 | tf_op jit(solution)/shard_map/ppermute | solution.py:130
  422.4 10.1 %collective-permute-done.39 = bf16[128,1536]{1,0:T(8,128)(2,1)S(1)} collective-permute-done((bf16[128,1536]{1,0:T(8,128)(2,1)S(1)}, bf16[128,1536]{1,0:T(8,128)(2,1)S(1)}, u32[]{:S(2)}, u32[]{:S(2)}) %collective-permute-start.39) | collective-permute-done | bytes 393248 | tf_op jit(solution)/shard_map/ppermute | solution.py:130
  433.5 5.0 %collective-permute-done.40 = bf16[64,1536]{1,0:T(8,128)(2,1)S(1)} collective-permute-done((bf16[64,1536]{1,0:T(8,128)(2,1)S(1)}, bf16[64,1536]{1,0:T(8,128)(2,1)S(1)}, u32[]{:S(2)}, u32[]{:S(2)}) %collective-permute-start.40) | collective-permute-done | bytes 196640 | tf_op jit(solution)/shard_map/ppermute | solution.py:130
  (412 shorter events, 125.1 us)
Async XLA Ops:
  1.7 15.3 %collective-permute-start.1 = (bf16[64,1536]{1,0:T(8,128)(2,1)S(1)}, bf16[64,1536]{1,0:T(8,128)(2,1)}, u32[]{:S(2)}, u32[]{:S(2)}) collective-permute-start(bf16[64,1536]{1,0:T(8,128)(2,1)S(1)} %bitcast.138), channel_id=1, source_target_pairs={{0,8},{2,10},{4,12},{6,14},{8,0},{10,2},{12,4},{14,6},{16,24},{18,... | collective-permute-start | bytes 589832 | tf_op jit(solution)/shard_map/ppermute | solution.py:130
  4.7 17.6 %collective-permute-start.15 = (bf16[64,2048]{1,0:T(8,128)(2,1)}, bf16[64,2048]{1,0:T(8,128)(2,1)S(1)}, u32[]{:S(2)}, u32[]{:S(2)}) collective-permute-start(bf16[64,2048]{1,0:T(8,128)(2,1)} %param.23), channel_id=1, source_target_pairs={{0,8},{2,10},{4,12},{6,14},{8,0},{10,2},{12,4},{14,6},{16,24},{18,... | collective-permute-start | bytes 786440 | tf_op jit(solution)/shard_map/ppermute | solution.py:130
  10.8 16.4 %collective-permute-start = (bf16[256,1024]{0,1:T(8,128)(2,1)}, bf16[256,1024]{0,1:T(8,128)(2,1)}, u32[]{:S(2)}, u32[]{:S(2)}) collective-permute-start(bf16[256,1024]{0,1:T(8,128)(2,1)} %add_convert_fusion.9), channel_id=1, source_target_pairs={{0,1},{1,0},{2,3},{3,2},{4,5},{5,4},{6,7},{7,6},{8,9},{9,8},{10,11... | collective-permute-start | bytes 1572872 | tf_op jit(solution)/shard_map/ppermute | solution.py:134
  12.2 13.4 %collective-permute-start.7 = (bf16[64,2560]{1,0:T(8,128)(2,1)S(1)}, bf16[64,2560]{1,0:T(8,128)(2,1)S(1)}, u32[]{:S(2)}, u32[]{:S(2)}) collective-permute-start(bf16[64,2560]{1,0:T(8,128)(2,1)S(1)} %get-tuple-element.193), channel_id=1, source_target_pairs={{0,8},{2,10},{4,12},{6,14},{8,0},{10,2},{12,4},{14,6},{16,24},{18,... | collective-permute-start | bytes 983048 | tf_op jit(solution)/shard_map/ppermute | solution.py:130
  18.0 46.7 %collective-permute-start.2 = (bf16[128,1536]{1,0:T(8,128)(2,1)S(1)}, bf16[128,1536]{1,0:T(8,128)(2,1)S(1)}, u32[]{:S(2)}, u32[]{:S(2)}) collective-permute-start(bf16[128,1536]{1,0:T(8,128)(2,1)S(1)} %pad_maximum_fusion.20), channel_id=1, source_target_pairs={{0,16},{2,18},{4,20},{6,22},{8,24},{10,26},{12,28},{14,30},{16,0},... | collective-permute-start | bytes 1179656 | tf_op jit(solution)/shard_map/ppermute | solution.py:130
  22.4 53.5 %collective-permute-start.16 = (bf16[128,2048]{1,0:T(8,128)(2,1)S(1)}, bf16[128,2048]{1,0:T(8,128)(2,1)S(1)}, u32[]{:S(2)}, u32[]{:S(2)}) collective-permute-start(bf16[128,2048]{1,0:T(8,128)(2,1)S(1)} %pad_maximum_fusion.19), channel_id=1, source_target_pairs={{0,16},{2,18},{4,20},{6,22},{8,24},{10,26},{12,28},{14,30},{16,0},... | collective-permute-start | bytes 1572872 | tf_op jit(solution)/shard_map/ppermute | solution.py:130
  25.7 63.6 %collective-permute-start.8 = (bf16[128,2560]{1,0:T(8,128)(2,1)S(1)}, bf16[128,2560]{1,0:T(8,128)(2,1)S(1)}, u32[]{:S(2)}, u32[]{:S(2)}) collective-permute-start(bf16[128,2560]{1,0:T(8,128)(2,1)S(1)} %pad_maximum_fusion.16), channel_id=1, source_target_pairs={{0,16},{2,18},{4,20},{6,22},{8,24},{10,26},{12,28},{14,30},{16,0},... | collective-permute-start | bytes 1966088 | tf_op jit(solution)/shard_map/ppermute | solution.py:130
  64.7 26.2 %collective-permute-start.4 = (bf16[256,1536]{1,0:T(8,128)(2,1)S(1)}, bf16[256,1536]{1,0:T(8,128)(2,1)S(1)}, u32[]{:S(2)}, u32[]{:S(2)}) collective-permute-start(bf16[256,1536]{1,0:T(8,128)(2,1)S(1)} %get-tuple-element.185), channel_id=1, source_target_pairs={{0,4},{2,6},{4,0},{6,2},{8,12},{10,14},{12,8},{14,10},{16,20},{18,... | collective-permute-start | bytes 2359304 | tf_op jit(solution)/shard_map/ppermute | solution.py:130
  66.3 26.3 %collective-permute-start.3 = (bf16[256,1536]{1,0:T(8,128)(2,1)S(1)}, bf16[256,1536]{1,0:T(8,128)(2,1)S(1)}, u32[]{:S(2)}, u32[]{:S(2)}) collective-permute-start(bf16[256,1536]{1,0:T(8,128)(2,1)S(1)} %get-tuple-element.185), channel_id=1, source_target_pairs={{0,2},{2,0},{4,6},{6,4},{8,10},{10,8},{12,14},{14,12},{16,18},{18,... | collective-permute-start | bytes 2359304 | tf_op jit(solution)/shard_map/ppermute | solution.py:130
  77.0 95.5 %collective-permute-start.18 = (bf16[256,2048]{1,0:T(8,128)(2,1)}, bf16[256,2048]{1,0:T(8,128)(2,1)}, u32[]{:S(2)}, u32[]{:S(2)}) collective-permute-start(bf16[256,2048]{1,0:T(8,128)(2,1)} %get-tuple-element.183), channel_id=1, source_target_pairs={{0,4},{2,6},{4,0},{6,2},{8,12},{10,14},{12,8},{14,10},{16,20},{18,... | collective-permute-start | bytes 3145736 | tf_op jit(solution)/shard_map/ppermute | solution.py:130
  78.5 95.6 %collective-permute-start.17 = (bf16[256,2048]{1,0:T(8,128)(2,1)}, bf16[256,2048]{1,0:T(8,128)(2,1)}, u32[]{:S(2)}, u32[]{:S(2)}) collective-permute-start(bf16[256,2048]{1,0:T(8,128)(2,1)} %get-tuple-element.183), channel_id=1, source_target_pairs={{0,2},{2,0},{4,6},{6,4},{8,10},{10,8},{12,14},{14,12},{16,18},{18,... | collective-permute-start | bytes 3145736 | tf_op jit(solution)/shard_map/ppermute | solution.py:130
  89.3 63.6 %collective-permute-start.10 = (bf16[256,2560]{1,0:T(8,128)(2,1)S(1)}, bf16[256,2560]{1,0:T(8,128)(2,1)S(1)}, u32[]{:S(2)}, u32[]{:S(2)}) collective-permute-start(bf16[256,2560]{1,0:T(8,128)(2,1)S(1)} %pad_maximum_fusion.5), channel_id=1, source_target_pairs={{0,4},{2,6},{4,0},{6,2},{8,12},{10,14},{12,8},{14,10},{16,20},{18,... | collective-permute-start | bytes 3932168 | tf_op jit(solution)/shard_map/ppermute | solution.py:130
  91.0 24.1 %collective-permute-start.6 = (bf16[256,768]{1,0:T(8,128)(2,1)S(1)}, bf16[256,768]{1,0:T(8,128)(2,1)S(1)}, u32[]{:S(2)}, u32[]{:S(2)}) collective-permute-start(bf16[256,768]{1,0:T(8,128)(2,1)S(1)} %slice.571), channel_id=1, source_target_pairs={{0,2},{2,0},{4,6},{6,4},{8,10},{10,8},{12,14},{14,12},{16,18},{18,... | collective-permute-start | bytes 1179656 | tf_op jit(solution)/shard_map/ppermute | solution.py:130
  92.6 49.3 %collective-permute-start.5 = (bf16[256,768]{1,0:T(8,128)(2,1)S(1)}, bf16[256,768]{1,0:T(8,128)(2,1)S(1)}, u32[]{:S(2)}, u32[]{:S(2)}) collective-permute-start(bf16[256,768]{1,0:T(8,128)(2,1)S(1)} %slice.570), channel_id=1, source_target_pairs={{0,4},{2,6},{4,0},{6,2},{8,12},{10,14},{12,8},{14,10},{16,20},{18,... | collective-permute-start | bytes 1179656 | tf_op jit(solution)/shard_map/ppermute | solution.py:130
  115.1 39.4 %collective-permute-start.9 = (bf16[256,2560]{1,0:T(8,128)(2,1)S(1)}, bf16[256,2560]{1,0:T(8,128)(2,1)S(1)}, u32[]{:S(2)}, u32[]{:S(2)}) collective-permute-start(bf16[256,2560]{1,0:T(8,128)(2,1)S(1)} %pad_maximum_fusion.5), channel_id=1, source_target_pairs={{0,2},{2,0},{4,6},{6,4},{8,10},{10,8},{12,14},{14,12},{16,18},{18,... | collective-permute-start | bytes 3932168 | tf_op jit(solution)/shard_map/ppermute | solution.py:130
  152.9 14.5 %collective-permute-start.12 = (bf16[256,1280]{1,0:T(8,128)(2,1)S(1)}, bf16[256,1280]{1,0:T(8,128)(2,1)S(1)}, u32[]{:S(2)}, u32[]{:S(2)}) collective-permute-start(bf16[256,1280]{1,0:T(8,128)(2,1)S(1)} %slice.566), channel_id=1, source_target_pairs={{0,2},{2,0},{4,6},{6,4},{8,10},{10,8},{12,14},{14,12},{16,18},{18,... | collective-permute-start | bytes 1966088 | tf_op jit(solution)/shard_map/ppermute | solution.py:130
  154.5 14.2 %collective-permute-start.11 = (bf16[256,1280]{1,0:T(8,128)(2,1)S(1)}, bf16[256,1280]{1,0:T(8,128)(2,1)S(1)}, u32[]{:S(2)}, u32[]{:S(2)}) collective-permute-start(bf16[256,1280]{1,0:T(8,128)(2,1)S(1)} %slice.565), channel_id=1, source_target_pairs={{0,4},{2,6},{4,0},{6,2},{8,12},{10,14},{12,8},{14,10},{16,20},{18,... | collective-permute-start | bytes 1966088 | tf_op jit(solution)/shard_map/ppermute | solution.py:130
  173.5 14.4 %collective-permute-start.20 = (bf16[256,1024]{1,0:T(8,128)(2,1)S(1)}, bf16[256,1024]{1,0:T(8,128)(2,1)S(1)}, u32[]{:S(2)}, u32[]{:S(2)}) collective-permute-start(bf16[256,1024]{1,0:T(8,128)(2,1)S(1)} %slice.585), channel_id=1, source_target_pairs={{0,2},{2,0},{4,6},{6,4},{8,10},{10,8},{12,14},{14,12},{16,18},{18,... | collective-permute-start | bytes 1572872 | tf_op jit(solution)/shard_map/ppermute | solution.py:130
  175.2 14.1 %collective-permute-start.19 = (bf16[256,1024]{1,0:T(8,128)(2,1)S(1)}, bf16[256,1024]{1,0:T(8,128)(2,1)S(1)}, u32[]{:S(2)}, u32[]{:S(2)}) collective-permute-start(bf16[256,1024]{1,0:T(8,128)(2,1)S(1)} %slice.584), channel_id=1, source_target_pairs={{0,4},{2,6},{4,0},{6,2},{8,12},{10,14},{12,8},{14,10},{16,20},{18,... | collective-permute-start | bytes 1572872 | tf_op jit(solution)/shard_map/ppermute | solution.py:130
  180.7 8.7 %collective-permute-start.14 = (bf16[256,1024]{0,1:T(8,128)(2,1)S(1)}, bf16[256,1024]{0,1:T(8,128)(2,1)S(1)}, u32[]{:S(2)}, u32[]{:S(2)}) collective-permute-start(bf16[256,1024]{0,1:T(8,128)(2,1)S(1)} %add_convert_fusion.8), channel_id=1, source_target_pairs={{0,1},{1,0},{2,3},{3,2},{4,5},{5,4},{6,7},{7,6},{8,9},{9,8},{10,11... | collective-permute-start | bytes 1572872 | tf_op jit(solution)/shard_map/ppermute | solution.py:134
  196.1 18.2 %collective-permute-start.21 = (bf16[256,1024]{0,1:T(8,128)(2,1)}, bf16[256,1024]{0,1:T(8,128)(2,1)}, u32[]{:S(2)}, u32[]{:S(2)}) collective-permute-start(bf16[256,1024]{0,1:T(8,128)(2,1)} %convolution_convert_fusion.17), channel_id=1, source_target_pairs={{0,1},{1,0},{2,3},{3,2},{4,5},{5,4},{6,7},{7,6},{8,9},{9,8},{10,11... | collective-permute-start | bytes 1572872 | tf_op jit(solution)/shard_map/ppermute | solution.py:134
  249.2 8.5 %collective-permute-start.27 = (bf16[256,1024]{0,1:T(8,128)(2,1)S(1)}, bf16[256,1024]{0,1:T(8,128)(2,1)S(1)}, u32[]{:S(2)}, u32[]{:S(2)}) collective-permute-start(bf16[256,1024]{0,1:T(8,128)(2,1)S(1)} %fusion.54), channel_id=1, source_target_pairs={{0,1},{1,0},{2,3},{3,2},{4,5},{5,4},{6,7},{7,6},{8,9},{9,8},{10,11... | collective-permute-start | bytes 1572872 | tf_op jit(solution)/shard_map/ppermute | solution.py:134
  250.0 31.0 %collective-permute-start.47 = (bf16[256,1024]{1,0:T(8,128)(2,1)S(1)}, bf16[256,1024]{1,0:T(8,128)(2,1)S(1)}, u32[]{:S(2)}, u32[]{:S(2)}) collective-permute-start(bf16[256,1024]{1,0:T(8,128)(2,1)S(1)} %get-tuple-element.169), channel_id=1, source_target_pairs={{0,4},{2,6},{4,0},{6,2},{8,12},{10,14},{12,8},{14,10},{16,20},{18,... | collective-permute-start | bytes 1572872 | tf_op jit(solution)/shard_map/ppermute | solution.py:130
  251.6 30.7 %collective-permute-start.49 = (bf16[256,1024]{1,0:T(8,128)(2,1)S(1)}, bf16[256,1024]{1,0:T(8,128)(2,1)S(1)}, u32[]{:S(2)}, u32[]{:S(2)}) collective-permute-start(bf16[256,1024]{1,0:T(8,128)(2,1)S(1)} %get-tuple-element.170), channel_id=1, source_target_pairs={{0,2},{2,0},{4,6},{6,4},{8,10},{10,8},{12,14},{14,12},{16,18},{18,... | collective-permute-start | bytes 1572872 | tf_op jit(solution)/shard_map/ppermute | solution.py:130
  253.2 25.0 %collective-permute-start.53 = (bf16[256,1024]{1,0:T(8,128)(2,1)S(1)}, bf16[256,1024]{1,0:T(8,128)(2,1)S(1)}, u32[]{:S(2)}, u32[]{:S(2)}) collective-permute-start(bf16[256,1024]{1,0:T(8,128)(2,1)S(1)} %get-tuple-element.167), channel_id=1, source_target_pairs={{0,4},{2,6},{4,0},{6,2},{8,12},{10,14},{12,8},{14,10},{16,20},{18,... | collective-permute-start | bytes 1572872 | tf_op jit(solution)/shard_map/ppermute | solution.py:130
  253.7 22.7 %collective-permute-start.55 = (bf16[256,1024]{1,0:T(8,128)(2,1)S(1)}, bf16[256,1024]{1,0:T(8,128)(2,1)S(1)}, u32[]{:S(2)}, u32[]{:S(2)}) collective-permute-start(bf16[256,1024]{1,0:T(8,128)(2,1)S(1)} %get-tuple-element.168), channel_id=1, source_target_pairs={{0,2},{2,0},{4,6},{6,4},{8,10},{10,8},{12,14},{14,12},{16,18},{18,... | collective-permute-start | bytes 1572872 | tf_op jit(solution)/shard_map/ppermute | solution.py:130
  261.8 21.7 %collective-permute-start.28 = (bf16[256,1024]{0,1:T(8,128)(2,1)S(1)}, bf16[256,1024]{0,1:T(8,128)(2,1)S(1)}, u32[]{:S(2)}, u32[]{:S(2)}) collective-permute-start(bf16[256,1024]{0,1:T(8,128)(2,1)S(1)} %multiply_convert_fusion.3), channel_id=1, source_target_pairs={{0,1},{1,0},{2,3},{3,2},{4,5},{5,4},{6,7},{7,6},{8,9},{9,8},{10,11... | collective-permute-start | bytes 1572872 | tf_op jit(solution)/shard_map/ppermute | solution.py:134
  277.7 57.1 %collective-permute-start.56 = (bf16[256,2048]{1,0:T(8,128)(2,1)}, bf16[256,2048]{1,0:T(8,128)(2,1)}, u32[]{:S(2)}, u32[]{:S(2)}) collective-permute-start(bf16[256,2048]{1,0:T(8,128)(2,1)} %pad_maximum_fusion.13), channel_id=1, source_target_pairs={{0,4},{2,6},{4,0},{6,2},{8,12},{10,14},{12,8},{14,10},{16,20},{18,... | collective-permute-start | bytes 3145736 | tf_op jit(solution)/shard_map/ppermute | solution.py:130
  279.4 57.3 %collective-permute-start.54 = (bf16[256,2048]{1,0:T(8,128)(2,1)}, bf16[256,2048]{1,0:T(8,128)(2,1)}, u32[]{:S(2)}, u32[]{:S(2)}) collective-permute-start(bf16[256,2048]{1,0:T(8,128)(2,1)} %pad_maximum_fusion.12), channel_id=1, source_target_pairs={{0,2},{2,0},{4,6},{6,4},{8,10},{10,8},{12,14},{14,12},{16,18},{18,... | collective-permute-start | bytes 3145736 | tf_op jit(solution)/shard_map/ppermute | solution.py:130
  303.6 23.8 %collective-permute-start.29 = (bf16[256,1024]{0,1:T(8,128)(2,1)S(1)}, bf16[256,1024]{0,1:T(8,128)(2,1)S(1)}, u32[]{:S(2)}, u32[]{:S(2)}) collective-permute-start(bf16[256,1024]{0,1:T(8,128)(2,1)S(1)} %convolution_convert_fusion.14), channel_id=1, source_target_pairs={{0,1},{1,0},{2,3},{3,2},{4,5},{5,4},{6,7},{7,6},{8,9},{9,8},{10,11... | collective-permute-start | bytes 1572872 | tf_op jit(solution)/shard_map/ppermute | solution.py:134
  306.5 9.3 %collective-permute-start.35 = (bf16[256,768]{1,0:T(8,128)(2,1)S(1)}, bf16[256,768]{1,0:T(8,128)(2,1)S(1)}, u32[]{:S(2)}, u32[]{:S(2)}) collective-permute-start(bf16[256,768]{1,0:T(8,128)(2,1)S(1)} %get-tuple-element.181), channel_id=1, source_target_pairs={{0,4},{2,6},{4,0},{6,2},{8,12},{10,14},{12,8},{14,10},{16,20},{18,... | collective-permute-start | bytes 1179656 | tf_op jit(solution)/shard_map/ppermute | solution.py:130
  308.1 9.3 %collective-permute-start.37 = (bf16[256,768]{1,0:T(8,128)(2,1)S(1)}, bf16[256,768]{1,0:T(8,128)(2,1)S(1)}, u32[]{:S(2)}, u32[]{:S(2)}) collective-permute-start(bf16[256,768]{1,0:T(8,128)(2,1)S(1)} %get-tuple-element.182), channel_id=1, source_target_pairs={{0,2},{2,0},{4,6},{6,4},{8,10},{10,8},{12,14},{14,12},{16,18},{18,... | collective-permute-start | bytes 1179656 | tf_op jit(solution)/shard_map/ppermute | solution.py:130
  315.8 7.4 %collective-permute-start.44 = (bf16[256,512]{1,0:T(8,128)(2,1)S(1)}, bf16[256,512]{1,0:T(8,128)(2,1)S(1)}, u32[]{:S(2)}, u32[]{:S(2)}) collective-permute-start(bf16[256,512]{1,0:T(8,128)(2,1)S(1)} %pad_maximum_fusion.26), channel_id=1, source_target_pairs={{0,4},{2,6},{4,0},{6,2},{8,12},{10,14},{12,8},{14,10},{16,20},{18,... | collective-permute-start | bytes 786440 | tf_op jit(solution)/shard_map/ppermute | solution.py:130
  317.4 8.2 %collective-permute-start.42 = (bf16[256,512]{1,0:T(8,128)(2,1)S(1)}, bf16[256,512]{1,0:T(8,128)(2,1)S(1)}, u32[]{:S(2)}, u32[]{:S(2)}) collective-permute-start(bf16[256,512]{1,0:T(8,128)(2,1)S(1)} %pad_maximum_fusion.25), channel_id=1, source_target_pairs={{0,2},{2,0},{4,6},{6,4},{8,10},{10,8},{12,14},{14,12},{16,18},{18,... | collective-permute-start | bytes 786440 | tf_op jit(solution)/shard_map/ppermute | solution.py:130
  323.2 26.5 %collective-permute-start.50 = (bf16[256,2048]{1,0:T(8,128)(2,1)}, bf16[256,2048]{1,0:T(8,128)(2,1)}, u32[]{:S(2)}, u32[]{:S(2)}) collective-permute-start(bf16[256,2048]{1,0:T(8,128)(2,1)} %pad_maximum_fusion.11), channel_id=1, source_target_pairs={{0,4},{2,6},{4,0},{6,2},{8,12},{10,14},{12,8},{14,10},{16,20},{18,... | collective-permute-start | bytes 3145736 | tf_op jit(solution)/shard_map/ppermute | solution.py:130
  325.6 26.4 %collective-permute-start.48 = (bf16[256,2048]{1,0:T(8,128)(2,1)}, bf16[256,2048]{1,0:T(8,128)(2,1)}, u32[]{:S(2)}, u32[]{:S(2)}) collective-permute-start(bf16[256,2048]{1,0:T(8,128)(2,1)} %pad_maximum_fusion.10), channel_id=1, source_target_pairs={{0,2},{2,0},{4,6},{6,4},{8,10},{10,8},{12,14},{14,12},{16,18},{18,... | collective-permute-start | bytes 3145736 | tf_op jit(solution)/shard_map/ppermute | solution.py:130
  327.4 7.2 %collective-permute-start.45 = (bf16[128,512]{1,0:T(8,128)(2,1)}, bf16[128,512]{1,0:T(8,128)(2,1)S(1)}, u32[]{:S(2)}, u32[]{:S(2)}) collective-permute-start(bf16[128,512]{1,0:T(8,128)(2,1)} %get-tuple-element.180), channel_id=1, source_target_pairs={{0,16},{2,18},{4,20},{6,22},{8,24},{10,26},{12,28},{14,30},{16,0},... | collective-permute-start | bytes 393224 | tf_op jit(solution)/shard_map/ppermute | solution.py:130
  334.6 77.1 %collective-permute-start.38 = (bf16[256,1536]{1,0:T(8,128)(2,1)}, bf16[256,1536]{1,0:T(8,128)(2,1)S(1)}, u32[]{:S(2)}, u32[]{:S(2)}) collective-permute-start(bf16[256,1536]{1,0:T(8,128)(2,1)} %pad_maximum_fusion.15), channel_id=1, source_target_pairs={{0,4},{2,6},{4,0},{6,2},{8,12},{10,14},{12,8},{14,10},{16,20},{18,... | collective-permute-start | bytes 2359304 | tf_op jit(solution)/shard_map/ppermute | solution.py:130
  334.8 76.9 %collective-permute-start.36 = (bf16[256,1536]{1,0:T(8,128)(2,1)}, bf16[256,1536]{1,0:T(8,128)(2,1)S(1)}, u32[]{:S(2)}, u32[]{:S(2)}) collective-permute-start(bf16[256,1536]{1,0:T(8,128)(2,1)} %pad_maximum_fusion.14), channel_id=1, source_target_pairs={{0,2},{2,0},{4,6},{6,4},{8,10},{10,8},{12,14},{14,12},{16,18},{18,... | collective-permute-start | bytes 2359304 | tf_op jit(solution)/shard_map/ppermute | solution.py:130
  336.7 49.5 %collective-permute-start.46 = (bf16[64,512]{1,0:T(8,128)(2,1)S(1)}, bf16[64,512]{1,0:T(8,128)(2,1)S(1)}, u32[]{:S(2)}, u32[]{:S(2)}) collective-permute-start(bf16[64,512]{1,0:T(8,128)(2,1)S(1)} %add_convert_fusion.28), channel_id=1, source_target_pairs={{0,8},{2,10},{4,12},{6,14},{8,0},{10,2},{12,4},{14,6},{16,24},{18,... | collective-permute-start | bytes 196616 | tf_op jit(solution)/shard_map/ppermute | solution.py:130
  354.7 7.2 %collective-permute-start.31 = (f32[8,640]{1,0:T(8,128)S(1)}, f32[8,640]{1,0:T(8,128)S(1)}, u32[]{:S(2)}, u32[]{:S(2)}) collective-permute-start(f32[8,640]{1,0:T(8,128)S(1)} %pad_maximum_fusion.27), channel_id=1, source_target_pairs={{0,4},{2,6},{4,0},{6,2},{8,12},{10,14},{12,8},{14,10},{16,20},{18,... | collective-permute-start | bytes 61448 | tf_op jit(solution)/shard_map/ppermute | solution.py:130
  364.0 35.8 %collective-permute-start.57 = (bf16[128,2048]{1,0:T(8,128)(2,1)S(1)}, bf16[128,2048]{1,0:T(8,128)(2,1)S(1)}, u32[]{:S(2)}, u32[]{:S(2)}) collective-permute-start(bf16[128,2048]{1,0:T(8,128)(2,1)S(1)} %get-tuple-element.152), channel_id=1, source_target_pairs={{0,16},{2,18},{4,20},{6,22},{8,24},{10,26},{12,28},{14,30},{16,0},... | collective-permute-start | bytes 1572872 | tf_op jit(solution)/shard_map/ppermute | solution.py:130
  366.3 19.7 %collective-permute-start.33 = (f32[8,256]{1,0:T(8,128)S(1)}, f32[8,256]{1,0:T(8,128)S(1)}, u32[]{:S(2)}, u32[]{:S(2)}) collective-permute-start(f32[8,256]{1,0:T(8,128)S(1)} %pad_maximum_fusion.29), channel_id=1, source_target_pairs={{0,16},{2,18},{4,20},{6,22},{8,24},{10,26},{12,28},{14,30},{16,0},... | collective-permute-start | bytes 24584 | tf_op jit(solution)/shard_map/ppermute | solution.py:130
  386.0 25.5 %collective-permute-start.51 = (bf16[128,2048]{1,0:T(8,128)(2,1)S(1)}, bf16[128,2048]{1,0:T(8,128)(2,1)S(1)}, u32[]{:S(2)}, u32[]{:S(2)}) collective-permute-start(bf16[128,2048]{1,0:T(8,128)(2,1)S(1)} %get-tuple-element.154), channel_id=1, source_target_pairs={{0,16},{2,18},{4,20},{6,22},{8,24},{10,26},{12,28},{14,30},{16,0},... | collective-permute-start | bytes 1572872 | tf_op jit(solution)/shard_map/ppermute | solution.py:130
  386.2 11.7 %collective-permute-start.34 = (f32[8,192]{1,0:T(8,128)S(1)}, f32[8,192]{1,0:T(8,128)S(1)}, u32[]{:S(2)}, u32[]{:S(2)}) collective-permute-start(f32[8,192]{1,0:T(8,128)S(1)} %pad_maximum_fusion.30), channel_id=1, source_target_pairs={{0,8},{2,10},{4,12},{6,14},{8,0},{10,2},{12,4},{14,6},{16,24},{18,... | collective-permute-start | bytes 18440 | tf_op jit(solution)/shard_map/ppermute | solution.py:130
  399.9 21.6 %collective-permute-start.58 = (bf16[64,2048]{1,0:T(8,128)(2,1)S(1)}, bf16[64,2048]{1,0:T(8,128)(2,1)S(1)}, u32[]{:S(2)}, u32[]{:S(2)}) collective-permute-start(bf16[64,2048]{1,0:T(8,128)(2,1)S(1)} %add_convert_fusion.14), channel_id=1, source_target_pairs={{0,8},{2,10},{4,12},{6,14},{8,0},{10,2},{12,4},{14,6},{16,24},{18,... | collective-permute-start | bytes 786440 | tf_op jit(solution)/shard_map/ppermute | solution.py:130
  411.6 21.0 %collective-permute-start.52 = (bf16[64,2048]{1,0:T(8,128)(2,1)S(1)}, bf16[64,2048]{1,0:T(8,128)(2,1)S(1)}, u32[]{:S(2)}, u32[]{:S(2)}) collective-permute-start(bf16[64,2048]{1,0:T(8,128)(2,1)S(1)} %add_convert_fusion.16), channel_id=1, source_target_pairs={{0,8},{2,10},{4,12},{6,14},{8,0},{10,2},{12,4},{14,6},{16,24},{18,... | collective-permute-start | bytes 786440 | tf_op jit(solution)/shard_map/ppermute | solution.py:130
  412.0 20.4 %collective-permute-start.39 = (bf16[128,1536]{1,0:T(8,128)(2,1)S(1)}, bf16[128,1536]{1,0:T(8,128)(2,1)S(1)}, u32[]{:S(2)}, u32[]{:S(2)}) collective-permute-start(bf16[128,1536]{1,0:T(8,128)(2,1)S(1)} %get-tuple-element.158), channel_id=1, source_target_pairs={{0,16},{2,18},{4,20},{6,22},{8,24},{10,26},{12,28},{14,30},{16,0},... | collective-permute-start | bytes 1179656 | tf_op jit(solution)/shard_map/ppermute | solution.py:130
  (92 other events, 1358.0 us)
